TPU v7x, 256 devices: a whole 4x4x8 slice. The times are simulated.
256 devices in a mesh: occ: 64 (over z, y, core), ao: 4 (over x).
Axes of the slice: x: 4, y: 4, z: 8, core: 2. Of those that a mesh axis runs over, the one named last changes fastest.
Arguments:
- amplitudes: bfloat16 [256, 256, 256], P('occ', None, 'ao'), may hold values from -6 to 6
- orbitals: bfloat16 [512, 256], replicated, may hold values from -0.375 to 0.375
- tiles: bfloat16 [4096, 512, 512], P('occ', None, 'ao'), may hold values from -0.125 to 0.125
- tile_count: int32 [64], replicated, may hold values from 1 to 64, 2048 in all
- tile_row: int32 [4096], replicated, may hold values from 0 to 7
- tile_src: int32 [4096, 1], replicated, may hold values from 0 to 63; in each aligned block of 64 rows (0 to 63, 64 to 127, ...) at most 2 rows name the same one
- tile_sub: int32 [4096], replicated, may hold values from 0 to 7
Outputs:
- sigma_out: bfloat16 [256, 256, 256], P('occ', None, 'ao')
Inputs may be any that keep to these rules, and one draw needn't show every extreme that they name: `tile_count`: each occ index owns between 1 and 64 live slots, the first ones of its 64 slots; some index owns exactly 64. `tile_src`: among the 64 slots of one owner no source index is named more than 2 times, and some owner names one source exactly 2 times.
All inputs are finite; a program needn't handle non-finite values.
Results may differ from a plain program's by a relative error of at most 0.024.
Values may be sent and summed in bfloat16 or wider, within the bound.
A program may use at most 128 MiB of HBM per device.

v0:
```python
import jax
import jax.numpy as jnp
from jax import lax
from jax.sharding import PartitionSpec as P


def shards(amplitudes, orbitals, tiles, tile_count, tile_row, tile_src, tile_sub):
    node_count = lax.axis_size("occ")
    own_index = lax.axis_index("occ")
    quarter = lax.axis_index("ao")
    local_occ, vir_count, vir_part = amplitudes.shape
    ao_count = orbitals.shape[0]
    ao_part = ao_count // lax.axis_size("ao")
    slot_count = tiles.shape[0]
    blocks = ao_count // node_count
    nu_rows = lax.dynamic_slice_in_dim(orbitals, quarter * ao_part, ao_part, 0)
    vir_cols = lax.dynamic_slice_in_dim(orbitals, quarter * vir_part, vir_part, 1)
    partial_x = jnp.einsum("icd,nd->icn", amplitudes, vir_cols, preferred_element_type=jnp.float32)
    half_pairs = lax.psum_scatter(
        partial_x.astype(jnp.bfloat16), "ao", scatter_dimension=2, tiled=True
    )
    pair_rows = jnp.einsum(
        "mc,icn->imn", orbitals, half_pairs, preferred_element_type=jnp.float32
    ).astype(jnp.bfloat16)
    sources = tile_src[:, 0].reshape(node_count, slot_count)
    sub_blocks = tile_sub.reshape(node_count, slot_count)
    own_src = lax.dynamic_index_in_dim(sources, own_index, 0, keepdims=False)
    home_rows = lax.all_to_all(pair_rows, "occ", split_axis=1, concat_axis=0, tiled=True)
    per_peer = max(2, (slot_count + node_count - 1) // node_count)
    matches = sources == own_index
    send_rank = jnp.cumsum(matches.astype(jnp.int32), axis=1) - 1
    levels = jnp.arange(per_peer, dtype=jnp.int32)
    chosen = matches[:, None, :] & (send_rank[:, None, :] == levels[None, :, None])
    block_id = jnp.sum(jnp.where(chosen, sub_blocks[:, None, :], 0), axis=2)
    all_occ = home_rows.shape[0]
    packed = jnp.take(home_rows, block_id.reshape(-1), axis=1).reshape(
        all_occ, node_count, per_peer, ao_part
    )
    arrived = lax.all_to_all(packed, "occ", split_axis=1, concat_axis=1, tiled=True)
    positions = jnp.arange(slot_count, dtype=jnp.int32)
    earlier = positions[:, None] > positions[None, :]
    same_src = own_src[:, None] == own_src[None, :]
    own_rank = jnp.sum((earlier & same_src).astype(jnp.int32), axis=1)
    fetched = jnp.take(
        arrived.reshape(all_occ, node_count * per_peer, ao_part),
        own_src * per_peer + own_rank,
        axis=1,
    )
    live_mask = jnp.arange(slot_count, dtype=jnp.int32) < tile_count[own_index]
    own_row = lax.dynamic_index_in_dim(
        tile_row.reshape(node_count, slot_count), own_index, 0, keepdims=False
    )
    onehot = (
        (own_row[:, None] == jnp.arange(blocks, dtype=jnp.int32)[None, :]) & live_mask[:, None]
    ).astype(jnp.bfloat16)
    products = jnp.einsum("itn,tsn->tis", fetched, tiles, preferred_element_type=jnp.float32)
    upper_part = products.astype(jnp.bfloat16)
    lower_part = (products - upper_part.astype(jnp.float32)).astype(jnp.bfloat16)
    partial_z = jnp.einsum("tr,tis->irs", onehot, upper_part, preferred_element_type=jnp.float32)
    partial_z = partial_z + jnp.einsum(
        "tr,tis->irs", onehot, lower_part, preferred_element_type=jnp.float32
    )
    ladder = lax.psum_scatter(partial_z.astype(jnp.bfloat16), "ao", scatter_dimension=2, tiled=True)
    back_rows = lax.all_to_all(ladder, "occ", split_axis=0, concat_axis=1, tiled=True)
    mixed = jnp.einsum(
        "la,ils->ias", orbitals, back_rows, preferred_element_type=jnp.float32
    ).astype(jnp.bfloat16)
    partial_s = jnp.einsum("ias,sb->iab", mixed, nu_rows, preferred_element_type=jnp.float32)
    return lax.psum_scatter(partial_s.astype(jnp.bfloat16), "ao", scatter_dimension=2, tiled=True)


def solution(mesh):
    placed = (P("occ", None, "ao"), P(), P("occ", None, "ao"), P(), P(), P(), P())
    return jax.shard_map(
        shards, mesh=mesh, in_specs=placed, out_specs=P("occ", None, "ao"), check_vma=False
    )
```

profile of v0, /device:TPU:1, one launch (start us, length us, event | category | flops | bytes accessed | tf_op | source)
XLA Modules:
  0.0 508.1 jit_solution(4199454795965634853)
XLA Ops:
  7.5 2.4 fusion.12
  10.4 1.4 reduce.3
  11.9 26.7 %reduce-scatter.6.cloned.1.call-done = bf16[4,256,128]{1,2,0:T(8,128)(2,1)} async-done(((bf16[4,256,512]{1,2,0:T(8,128)(2,1)}), bf16[4,256,128]{1,2,0:T(8,128)(2,1)}) %reduce-scatter.6.cloned.1.call-update) | async-done | bytes 262160 | tf_op jit(solution)/shard_map/reduce_scatter | solution.py:19
  38.6 1.3 fusion.13
  39.9 1.1 copy.41
  41.0 12.1 %all-to-all-start = ((bf16[4,512,128]{2,0,1:T(4,128)(2,1)}), bf16[4,512,128]{2,0,1:T(4,128)(2,1)S(1)}, u32[]{:S(2)}, u32[]{:S(2)}) async-start(bf16[4,512,128]{2,0,1:T(4,128)(2,1)} %copy.41), calls=%async_computation.1 | async-start | bytes 1048576 | tf_op jit(solution)/shard_map/all_to_all | solution.py:28
  54.7 16.1 %all-to-all-done = bf16[4,512,128]{2,0,1:T(4,128)(2,1)S(1)} async-done(((bf16[4,512,128]{2,0,1:T(4,128)(2,1)}), bf16[4,512,128]{2,0,1:T(4,128)(2,1)S(1)}, u32[]{:S(2)}, u32[]{:S(2)}) %all-to-all-start) | async-done | bytes 524320 | tf_op jit(solution)/shard_map/all_to_all | solution.py:28
  71.0 6.4 %gather_fusion = bf16[128,256,128]{2,1,0:T(8,128)(2,1)} fusion(bf16[256,8,128]{2,0,1:T(8,128)(2,1)S(1)} %copy.45, s32[1024]{0:T(1024)S(1)} %pad_clamp_fusion.1), kind=kCustom, calls=%fused_computation | custom fusion | bytes 16777728 | tf_op jit(solution)/shard_map/jit(_take)/gather | solution.py:36
  77.4 7.4 %broadcast_select_fusion = bf16[256,64,2,128]{3,0,2,1:T(8,128)(2,1)} fusion(bf16[256,64,2,128]{3,0,2,1:T(8,128)(2,1)} %bitcast.74, pred[64,2]{1,0:T(8,128)(4,1)S(1)} %copy.39), kind=kLoop, calls=%fused_computation.7 | loop fusion | flops 4194304 | bytes 16777344 | tf_op jit(solution)/shard_map/jit(_take)/select_n | solution.py:36
  84.9 6.0 %all-to-all-start.1 = ((bf16[256,64,2,128]{3,0,2,1:T(8,128)(2,1)}), bf16[256,64,2,128]{3,0,2,1:T(8,128)(2,1)}, u32[]{:S(2)}, u32[]{:S(2)}) async-start(bf16[256,64,2,128]{3,0,2,1:T(8,128)(2,1)} %broadcast_select_fusion), calls=%async_computation.2 | async-start | bytes 16777216 | tf_op jit(solution)/shard_map/all_to_all | solution.py:39
  92.7 180.5 %all-to-all-done.1 = bf16[256,64,2,128]{3,0,2,1:T(8,128)(2,1)} async-done(((bf16[256,64,2,128]{3,0,2,1:T(8,128)(2,1)}), bf16[256,64,2,128]{3,0,2,1:T(8,128)(2,1)}, u32[]{:S(2)}, u32[]{:S(2)}) %all-to-all-start.1) | async-done | bytes 8388640 | tf_op jit(solution)/shard_map/all_to_all | solution.py:39
  273.1 6.5 %gather_fusion.1 = bf16[64,256,128]{2,1,0:T(8,128)(2,1)} fusion(bf16[256,128,128]{2,0,1:T(8,128)(2,1)} %bitcast.11, s32[1024]{0:T(1024)S(1)} %pad_clamp_fusion), kind=kCustom, calls=%fused_computation.1 | custom fusion | bytes 8388864 | tf_op jit(solution)/shard_map/jit(_take)/gather | solution.py:44
  279.7 19.5 %subtract_convert_fusion = (bf16[64,256,512]{2,1,0:T(8,128)(2,1)}, bf16[64,256,512]{2,1,0:T(8,128)(2,1)}) fusion(bf16[64,512,128]{2,1,0:T(8,128)(2,1)} %param.9, bf16[64,256,128]{2,1,0:T(8,128)(2,1)} %gather_fusion.1, pred[64]{0:T(512)(128)(4,1)S(1)} %compare_and_fusion.1), kind=kOutput, calls=%fused_computation.2 | convolution fusion | flops 2183135232 | bytes 46137408 | tf_op jit(solution)/shard_map/itn,tsn->tis/dot_general | solution.py:56
  299.1 16.7 %fusion = f32[256,512,8]{1,2,0:T(8,128)S(1)} fusion(bf16[64,256,512]{2,1,0:T(8,128)(2,1)} %get-tuple-element.5, s32[64]{0:T(128)S(1)} %fusion.38, pred[64]{0:T(512)(128)(4,1)S(1)} %iota_compare_fusion.3), kind=kOutput, calls=%fused_computation.3 | convolution fusion | flops 134218752 | bytes 20971840 | tf_op jit(solution)/shard_map/tr,tis->irs/dot_general | solution.py:60
  315.8 15.0 %fusion.8 = bf16[256,8,512]{2,1,0:T(8,128)(2,1)S(1)} fusion(f32[256,512,8]{1,2,0:T(8,128)S(1)} %fusion, bf16[64,256,512]{2,1,0:T(8,128)(2,1)} %get-tuple-element.6, s32[64]{0:T(128)S(1)} %fusion.38, pred[64]{0:T(512)(128)(4,1)S(1)} %iota_compare_fusion.3), kind=kOutput, calls=%fused_computation.13 | convolution fusion | flops 136315904 | bytes 23068992 | tf_op jit(solution)/shard_map/tr,tis->irs/dot_general | solution.py:59
  330.8 24.0 %copy.54 = bf16[256,8,512]{1,0,2:T(8,128)(2,1)} copy(bf16[256,8,512]{2,1,0:T(8,128)(2,1)S(1)} %fusion.8) | data formatting | bytes 4194304
  354.8 48.5 %reshape.130 = bf16[512,2048]{1,0:T(8,128)(2,1)} reshape(bf16[512,256,8]{2,1,0:T(8,128)(2,1)} %bitcast.73) | data formatting | bytes 4194304
  403.3 31.5 %reduce-scatter.10.cloned.1.call-done = bf16[128,2048]{1,0:T(8,128)(2,1)} async-done(((bf16[512,2048]{1,0:T(8,128)(2,1)}), bf16[128,2048]{1,0:T(8,128)(2,1)}) %reduce-scatter.10.cloned.1.call-update) | async-done | bytes 524304
  434.8 11.9 %reshape.131 = bf16[128,256,8]{2,1,0:T(8,128)(2,1)} reshape(bf16[128,2048]{1,0:T(8,128)(2,1)} %reduce-scatter.10.cloned.1.call-done) | data formatting | bytes 1048576
  446.6 8.2 %copy.55 = bf16[256,8,128]{2,1,0:T(8,128)(2,1)} copy(bf16[256,8,128]{1,0,2:T(8,128)(2,1)} %bitcast.75) | data formatting | bytes 1048576
  454.8 10.8 %all-to-all-start.2 = ((bf16[256,8,128]{2,1,0:T(8,128)(2,1)}), bf16[256,8,128]{2,1,0:T(8,128)(2,1)S(1)}, u32[]{:S(2)}, u32[]{:S(2)}) async-start(bf16[256,8,128]{2,1,0:T(8,128)(2,1)} %copy.55), calls=%async_computation.3 | async-start | bytes 1048576 | tf_op jit(solution)/shard_map/all_to_all | solution.py:64
  465.7 17.6 %all-to-all-done.2 = bf16[256,8,128]{2,1,0:T(8,128)(2,1)S(1)} async-done(((bf16[256,8,128]{2,1,0:T(8,128)(2,1)}), bf16[256,8,128]{2,1,0:T(8,128)(2,1)S(1)}, u32[]{:S(2)}, u32[]{:S(2)}) %all-to-all-start.2) | async-done | bytes 524320 | tf_op jit(solution)/shard_map/all_to_all | solution.py:64
  483.3 1.5 convolution_convert_fusion.2
  484.8 16.7 %reduce-scatter.8.cloned.1.call-done = bf16[4,256,64]{1,2,0:T(8,128)(2,1)} async-done(((bf16[4,256,256]{1,2,0:T(8,128)(2,1)}), bf16[4,256,64]{1,2,0:T(8,128)(2,1)}) %reduce-scatter.8.cloned.1.call-update) | async-done | bytes 131088 | tf_op jit(solution)/shard_map/reduce_scatter | solution.py:69
  (37 shorter events, 5.1 us)
Async XLA Ops:
  6.5 1.0 copy-start
  6.5 32.1 %reduce-scatter.6.cloned.1.call-start = ((), (), s32[]{:S(2)}) async-start(), calls=%async_computation.6 | async-start | bytes 1310720 | tf_op jit(solution)/shard_map/reduce_scatter | solution.py:19
  41.0 29.8 %all-to-all-start = ((bf16[4,512,128]{2,0,1:T(4,128)(2,1)}), bf16[4,512,128]{2,0,1:T(4,128)(2,1)S(1)}, u32[]{:S(2)}, u32[]{:S(2)}) async-start(bf16[4,512,128]{2,0,1:T(4,128)(2,1)} %copy.41), calls=%async_computation.1 | async-start | bytes 1048576 | tf_op jit(solution)/shard_map/all_to_all | solution.py:28
  84.8 6.2 %copy-start.1 = (s32[4096]{0:T(1024)S(1)}, s32[4096]{0:T(1024)}, u32[]{:S(2)}) copy-start(s32[4096]{0:T(1024)} %param.11) | copy-start | bytes 49156
  84.9 6.3 %copy-start.2 = (s32[64]{0:T(128)S(1)}, s32[64]{0:T(128)}, u32[]{:S(2)}) copy-start(s32[64]{0:T(128)} %param.10) | copy-start | bytes 772
  84.9 188.3 %all-to-all-start.1 = ((bf16[256,64,2,128]{3,0,2,1:T(8,128)(2,1)}), bf16[256,64,2,128]{3,0,2,1:T(8,128)(2,1)}, u32[]{:S(2)}, u32[]{:S(2)}) async-start(bf16[256,64,2,128]{3,0,2,1:T(8,128)(2,1)} %broadcast_select_fusion), calls=%async_computation.2 | async-start | bytes 16777216 | tf_op jit(solution)/shard_map/all_to_all | solution.py:39
  90.9 343.9 %reduce-scatter.10.cloned.1.call-start = ((), (), s32[]{:S(2)}) async-start(), calls=%async_computation.8 | async-start | bytes 2621440
  454.8 28.5 %all-to-all-start.2 = ((bf16[256,8,128]{2,1,0:T(8,128)(2,1)}), bf16[256,8,128]{2,1,0:T(8,128)(2,1)S(1)}, u32[]{:S(2)}, u32[]{:S(2)}) async-start(bf16[256,8,128]{2,1,0:T(8,128)(2,1)} %copy.55), calls=%async_computation.3 | async-start | bytes 1048576 | tf_op jit(solution)/shard_map/all_to_all | solution.py:64
  465.6 36.0 %reduce-scatter.8.cloned.1.call-start = ((), (), s32[]{:S(2)}) async-start(), calls=%async_computation.7 | async-start | bytes 655360 | tf_op jit(solution)/shard_map/reduce_scatter | solution.py:69
Sparse Core Ops, SparseCore 0:
  10.0 28.5 reduce-scatter.5
  403.4 31.3 reduce-scatter.9
  485.0 16.5 reduce-scatter.7
where the time goes:
time: 510 us; the launch traced here: 508 us
  waiting for transfers between devices  289 us (57%)
  local copies, waits for them, and re-layouts  110 us (22%)
  matrix products  56.3 us (11%)
  starting transfers between devices  29.2 us (6%)
  between operations  13.3 us (3%)
  other arithmetic  10 us (2%)
    all_to_all x1, waiting for transfers between devices, shards(): lax.all_to_all(packed, 'occ', split_axis=1, concat_axis=1, tiled=True)  180 us
    unnamed x11, local copies, waits for them, and re-layouts  93.9 us
    unnamed x4, waiting for transfers between devices  31.5 us
    reduce_scatter x1, waiting for transfers between devices, shards(): lax.psum_scatter(partial_x.astype(jnp.bfloat16), 'ao', scatter_dimension=...  26.7 us
    dot_general x1, matrix products, shards(): jnp.einsum('itn,tsn->tis', fetched, tiles, preferred_element_type=jnp.flo...  19.5 us
    all_to_all x1, waiting for transfers between devices, shards(): lax.all_to_all(ladder, 'occ', split_axis=0, concat_axis=1, tiled=True)  17.6 us
    reduce_scatter x1, waiting for transfers between devices, shards(): lax.psum_scatter(partial_s.astype(jnp.bfloat16), 'ao', scatter_dimension=...  16.7 us
    dot_general x1, matrix products, shards(): jnp.einsum('tr,tis->irs', onehot, lower_part, preferred_element_type=jnp....  16.7 us
  transfers between devices with their start and end apart: 6, of which 6 were waited for; matrix products, arithmetic and copies ran while one was open for 1% of the time, Pallas kernels for 0%

commit v1 on v0

v1 whole, which is shorter than its diff:
```python
import jax
import jax.numpy as jnp
from jax import lax
from jax.experimental import pallas as pl
from jax.experimental.pallas import tpu as pltpu
from jax.sharding import PartitionSpec as P

BF16, F32 = jnp.bfloat16, jnp.float32


def ladder_kernel(count, rows, pairs, tile, orb, out, acc):
    slot = pl.program_id(0)

    @pl.when(slot == 0)
    def _():
        acc[...] = jnp.zeros_like(acc)

    @pl.when(slot < count[0])
    def _():
        folded = jnp.dot(orb[...], tile[0], preferred_element_type=F32).astype(BF16)
        term = lax.dot_general(
            pairs[0], folded, (((1,), (1,)), ((), ())), preferred_element_type=F32
        )
        acc[rows[slot]] += term

    @pl.when(slot == pl.num_programs(0) - 1)
    def _():
        out[...] = acc[...].astype(BF16)


def ladder_rows(count, rows, pairs, tiles, orb_t, blocks):
    slots, ao, part = tiles.shape
    occ = pairs.shape[1]
    vir = orb_t.shape[0]

    def live(t, c, r):
        return (jnp.minimum(t, c[0] - 1), 0, 0)

    return pl.pallas_call(
        ladder_kernel,
        out_shape=jax.ShapeDtypeStruct((blocks, occ, vir), BF16),
        grid_spec=pltpu.PrefetchScalarGridSpec(
            num_scalar_prefetch=2,
            grid=(slots,),
            in_specs=[
                pl.BlockSpec((1, occ, part), live),
                pl.BlockSpec((1, ao, part), live),
                pl.BlockSpec((vir, ao), lambda t, c, r: (0, 0)),
            ],
            out_specs=pl.BlockSpec((blocks, occ, vir), lambda t, c, r: (0, 0, 0)),
            scratch_shapes=[pltpu.VMEM((blocks, occ, vir), F32)],
        ),
        cost_estimate=pl.CostEstimate(
            flops=2 * slots * vir * part * (ao + occ),
            bytes_accessed=2 * slots * part * (ao + occ),
            transcendentals=0,
        ),
    )(count, rows, pairs, tiles, orb_t)


def shards(amplitudes, orbitals, tiles, tile_count, tile_row, tile_src, tile_sub):
    owners = lax.axis_size("occ")
    me = lax.axis_index("occ")
    quarter = lax.axis_index("ao")
    ao_count = orbitals.shape[0]
    ao_part = ao_count // lax.axis_size("ao")
    slots = tiles.shape[0]
    blocks = ao_count // owners
    nu_rows = lax.dynamic_slice_in_dim(orbitals, quarter * ao_part, ao_part, 0)
    amps = lax.all_gather(amplitudes, "ao", axis=2, tiled=True)
    half = jnp.einsum("icd,nd->icn", amps, nu_rows, preferred_element_type=F32).astype(BF16)
    half_all = lax.all_gather(half, "occ", axis=0, tiled=True)
    src = lax.dynamic_slice_in_dim(tile_src[:, 0], me * slots, slots, 0)
    sub = lax.dynamic_slice_in_dim(tile_sub, me * slots, slots, 0)
    row = lax.dynamic_slice_in_dim(tile_row, me * slots, slots, 0)
    count = lax.dynamic_slice_in_dim(tile_count, me, 1, 0)
    chosen = jnp.take(orbitals, src * blocks + sub, axis=0)
    pairs = jnp.einsum("tc,icn->tin", chosen, half_all, preferred_element_type=F32).astype(BF16)
    part = ladder_rows(count, row, pairs, tiles, orbitals.T, blocks)
    ladder = lax.psum_scatter(part, "ao", scatter_dimension=2, tiled=True)
    back = lax.all_to_all(ladder, "occ", split_axis=1, concat_axis=0, tiled=True)
    return jnp.einsum("la,lib->iab", orbitals, back, preferred_element_type=F32).astype(BF16)


def solution(mesh):
    placed = (P("occ", None, "ao"), P(), P("occ", None, "ao"), P(), P(), P(), P())
    return jax.shard_map(
        shards, mesh=mesh, in_specs=placed, out_specs=P("occ", None, "ao"), check_vma=False
    )
```

time: 510 us -> 248 us (0.49)
  waiting for transfers between devices: 289 us -> 153 us
  local copies, waits for them, and re-layouts: 110 us -> 16.1 us
  matrix products: 56.3 us -> 10.9 us
  blocking collectives: 0 us -> 37.5 us
  starting transfers between devices: 29.2 us -> 0.04 us
  Pallas kernels: 0 us -> 14.1 us
  other arithmetic: 10 us -> 0.77 us
    all_to_all x3 -> x0, waiting for transfers between devices: 214 us -> none  [the longest x1 180 us: shards(): lax.all_to_all(packed, 'occ', split_axis=1, concat_axis=1, tiled=True)]
    all_gather x0 -> x1, waiting for transfers between devices: none -> 97.7 us  [shards(): half_all = lax.all_gather(half, 'occ', axis=0, tiled=True)]
    unnamed x11 -> x5, local copies, waits for them, and re-layouts: 93.9 us -> 2.44 us
    dot_general x6 -> x3, matrix products: 56.3 us -> 10.9 us  [the longest x1 8.88 us: shards(): jnp.einsum('tc,icn->tin', chosen, half_all, preferred_element_type=F32)]
    unnamed x4 -> x2, waiting for transfers between devices: 31.5 us -> 0.03 us
    all_to_all x3 -> x0, starting transfers between devices: 28.9 us -> none  [the longest x1 12.1 us: shards(): lax.all_to_all(pair_rows, 'occ', split_axis=1, concat_axis=0, tiled=True)]
    all_to_all x0 -> x1, blocking collectives: none -> 25.1 us  [shards(): lax.all_to_all(ladder, 'occ', split_axis=1, concat_axis=0, tiled=True)]
    pallas_call x0 -> x1, Pallas kernels: none -> 14.1 us  [ladder_rows(): pl.pallas_call(ladder_kernel, out_shape=jax.ShapeDtypeStruct((blocks, occ...]
  transfers between devices with their start and end apart: 6 -> 2, of which waited for: 6 -> 2; matrix products, arithmetic and copies ran while one was open for 1% -> 3% of each run, Pallas kernels for 0% -> 0%
where the time goes in v1:
time: 248 us; the launch traced here: 246 us
  waiting for transfers between devices  153 us (62%)
  blocking collectives  37.5 us (15%)
  local copies, waits for them, and re-layouts  16.1 us (6%)
  Pallas kernels  14.1 us (6%)
  between operations  13.5 us (5%)
  matrix products  10.9 us (4%)
    all_gather x1, waiting for transfers between devices, shards(): half_all = lax.all_gather(half, 'occ', axis=0, tiled=True)  97.7 us
    reduce_scatter x1, waiting for transfers between devices, shards(): ladder = lax.psum_scatter(part, 'ao', scatter_dimension=2, tiled=True)  55.7 us
    all_to_all x1, blocking collectives, shards(): lax.all_to_all(ladder, 'occ', split_axis=1, concat_axis=0, tiled=True)  25.1 us
    pallas_call x1, Pallas kernels, ladder_rows(): pl.pallas_call(ladder_kernel, out_shape=jax.ShapeDtypeStruct((blocks, occ...  14.1 us
    all_gather x1, blocking collectives, shards(): amps = lax.all_gather(amplitudes, 'ao', axis=2, tiled=True)  12.5 us
    dot_general x1, matrix products, shards(): jnp.einsum('tc,icn->tin', chosen, half_all, preferred_element_type=F32)  8.88 us
  transfers between devices with their start and end apart: 2, of which 2 were waited for; matrix products, arithmetic and copies ran while one was open for 3% of the time, Pallas kernels for 0%

profile of v1, /device:TPU:1, one launch (start us, length us, event | category | flops | bytes accessed | tf_op | source)
XLA Modules:
  0.0 246.4 jit_solution(12969151570945607288)
XLA Ops:
  6.5 0.0 all-gather.2.cloned.1.call-start
  6.5 12.5 %all_gather.6 = bf16[4,256,256]{1,2,0:T(8,128)(2,1)S(1)} all-gather(bf16[4,256,64]{1,2,0:T(8,128)(2,1)} %param.7), channel_id=1, replica_groups=mesh['occ'=64,'ao'=4] {'ao'}, dimensions={2}, use_global_device_ids=true | all-gather | bytes 655360 | tf_op jit(solution)/shard_map/all_gather | solution.py:70
  19.0 1.1 fusion
  20.1 0.8 copy.15
  20.9 0.0 all-gather.2.cloned.1.call-update
  21.0 0.0 reduce-scatter.2.cloned.1.call-start
  21.0 1.8 copy.17
  22.8 0.8 compare_and_fusion
  23.6 1.6 gather_fusion
  25.2 1.3 dynamic_slice.16.rows
  26.5 1.2 dynamic_slice.15.count
  27.7 97.7 %all-gather.2.cloned.1.call-done = bf16[256,256,128]{2,1,0:T(8,128)(2,1)} async-done(((bf16[4,256,128]{2,1,0:T(8,128)(2,1)}), bf16[256,256,128]{2,1,0:T(8,128)(2,1)}) %all-gather.2.cloned.1.call-update) | async-done | bytes 16777232 | tf_op jit(solution)/shard_map/all_gather | solution.py:72
  125.4 8.9 %fusion.7 = bf16[64,256,128]{2,0,1:T(8,128)(2,1)S(1)} fusion(bf16[256,256,128]{2,1,0:T(8,128)(2,1)} %all-gather.2.cloned.1.call-done, bf16[64,256]{1,0:T(8,128)(2,1)S(1)} %gather_fusion, pred[64]{0:T(512)(128)(4,1)S(1)} %get-tuple-element.5), kind=kOutput, calls=%fused_computation.11 | convolution fusion | flops 1073758208 | bytes 21004352 | tf_op jit(solution)/shard_map/tc,icn->tin/dot_general | solution.py:78
  134.3 0.0 copy-start
  134.3 4.6 %copy.28.pairs = bf16[64,256,128]{2,1,0:T(8,128)(2,1)} copy(bf16[64,256,128]{2,0,1:T(8,128)(2,1)S(1)} %fusion.7) | data formatting | bytes 8388608 | tf_op jit(solution)/shard_map/tc,icn->tin/dot_general | solution.py:78
  138.9 14.1 %shard_map.73 = bf16[8,256,256]{2,1,0:T(8,128)(2,1)} custom-call(s32[1]{0:T(128)} %dynamic_slice.15.count, s32[64]{0:T(128)} %dynamic_slice.16.rows, bf16[64,256,128]{2,1,0:T(8,128)(2,1)} %copy.28.pairs, bf16[64,512,128]{2,1,0:T(8,128)(2,1)} %tile.1, bf16[256,512]{1,0:T(8,128)(2,1)} %bitcast.31), custom_call_target="tpu_custom_call" | custom-call | flops 3221225472 | bytes 12582912 | tf_op jit(solution)/shard_map/pallas_call | solution.py:39
  153.1 2.6 %copy.18 = bf16[8,256,256]{1,0,2:T(8,128)(2,1)} copy(bf16[8,256,256]{2,1,0:T(8,128)(2,1)} %shard_map.73) | data formatting | bytes 2097152 | tf_op jit(solution)/shard_map/pallas_call | solution.py:39
  155.7 0.0 reduce-scatter.2.cloned.1.call-update
  155.7 55.7 %reduce-scatter.2.cloned.1.call-done = bf16[8,256,64]{1,0,2:T(8,128)(2,1)} async-done(((bf16[8,256,256]{1,0,2:T(8,128)(2,1)}), bf16[8,256,64]{1,0,2:T(8,128)(2,1)}) %reduce-scatter.2.cloned.1.call-update) | async-done | bytes 262160 | tf_op jit(solution)/shard_map/reduce_scatter | solution.py:80
  211.4 1.4 copy.19
  212.8 0.3 reshape.20
  213.1 25.1 %all_to_all.18 = bf16[64,2,1024]{2,1,0:T(2,128)(2,1)S(1)} all-to-all(bf16[64,2,1024]{2,1,0:T(2,128)(2,1)S(1)} %reshape.20), channel_id=1, replica_groups=mesh['occ'=64,'ao'=4] {'occ'}, dimensions={0} | all-to-all | bytes 524288 | tf_op jit(solution)/shard_map/all_to_all | solution.py:81
  238.2 0.3 reshape.21
  238.6 1.0 fusion.1
  (2 shorter events, 0.0 us)
Async XLA Ops:
  6.5 118.9 %all-gather.2.cloned.1.call-start = ((), (), s32[]{:S(2)}) async-start(), calls=%async_computation.2 | async-start | bytes 17039360 | tf_op jit(solution)/shard_map/all_gather | solution.py:72
  21.0 190.4 %reduce-scatter.2.cloned.1.call-start = ((), (), s32[]{:S(2)}) async-start(), calls=%async_computation.3 | async-start | bytes 1310720 | tf_op jit(solution)/shard_map/reduce_scatter | solution.py:80
  134.3 104.2 %copy-start = (bf16[512,256]{1,0:T(8,128)(2,1)S(1)}, bf16[512,256]{1,0:T(8,128)(2,1)}, u32[]{:S(2)}) copy-start(bf16[512,256]{1,0:T(8,128)(2,1)} %param.8) | copy-start | bytes 786436
Sparse Core Ops, SparseCore 0:
  21.1 104.2 all-gather.1
  155.8 55.4 reduce-scatter.1

commit v2 on v1

v2 whole, which is shorter than its diff:
```python
import functools
import heapq
import itertools

import jax
import jax.numpy as jnp
from jax import lax
from jax.experimental import pallas as pl
from jax.experimental.pallas import tpu as pltpu
from jax.sharding import PartitionSpec as P

BF16, F32 = jnp.bfloat16, jnp.float32
MESH = pl.DeviceIdType.MESH
ZN, YN, XN = 8, 4, 4
NDEV = ZN * YN * 2
ROWS = 512
CUT = {"P": (0, 160, 304), "Q": (304, 416, 512)}
CLS = {"P": 0, "Q": 1}
ROW_ORDER = (0, 1, 7, 2, 6, 3, 5, 4)
SLOTS, NU, AO, VIR = 64, 128, 512, 256
USTEPS, PSTEPS, KSTEPS = 8, 4, 8
GSTEPS = PSTEPS + KSTEPS
GROUP = 32


def extent(cls, part):
    lo, mid, hi = CUT[cls]
    return {"f": (lo, hi - lo), "a": (lo, mid - lo), "b": (mid, hi - mid)}[part]


def route(rate=91e3, latency=1.7):
    free = {("z", 1): 0.0, ("z", -1): 0.0, ("y", 1): 0.0, ("y", -1): 0.0}
    tick = itertools.count()
    events, log, halves = [], [], {}

    def emit(now, cls, dz, dy, sends):
        for axis, way, part in sends:
            start = max(now, free[axis, way])
            free[axis, way] = start + 2 * 512 * extent(cls, part)[1] / rate
            at = ((dz - way) % ZN, dy) if axis == "z" else (dz, (dy - way) % YN)
            heapq.heappush(
                events, (free[axis, way] + latency, next(tick), cls, *at, part, axis, way)
            )

    for cls, axis in (("P", "z"), ("Q", "y"), ("P", "y"), ("Q", "z")):
        sends = [(axis, 1, "f"), (axis, -1, "f")]
        log.append((0.0, "own", cls, 0, 0, sends, axis == ("z" if cls == "P" else "y")))
        emit(0.0, cls, 0, 0, sends)
    while events:
        now, _, cls, dz, dy, part, axis, way = heapq.heappop(events)
        n = ZN if axis == "z" else YN
        gone = (-way * (dz if axis == "z" else dy)) % n
        sends = []
        if gone < n // 2 - 1:
            sends.append((axis, way, "f"))
        elif gone == n // 2 - 1:
            sends.append((axis, way, "a" if way == 1 else "b"))
        whole = part == "f"
        if not whole:
            seen = halves.setdefault((cls, dz, dy), set())
            seen.add(part)
            whole = len(seen) == 2
        if whole and axis == ("z" if cls == "P" else "y"):
            other = "y" if cls == "P" else "z"
            sends += [(other, 1, "f"), (other, -1, "f")]
        log.append((now, part, cls, dz, dy, sends, whole))
        emit(now, cls, dz, dy, sends)
    return log


def slots_of(log):
    table = [[] for _ in range(USTEPS + len(ROW_ORDER) * GSTEPS)]
    now, left = 0.0, list(range(len(log)))

    def take(step, test):
        nonlocal left
        table[step] += [e for e in left if test(log[e])]
        left = [e for e in left if not test(log[e])]

    for step in range(USTEPS):
        take(step, lambda e: e[0] <= now)
        now += 0.8
    for g, dz in enumerate(ROW_ORDER):
        ready = max(e[0] for e in log if e[3] == dz)
        for k in range(GSTEPS):
            step = USTEPS + g * GSTEPS + k
            if k == 0:
                now = max(now, ready)
            take(step, lambda e: e[0] <= now)
            now += 0.5 if k < PSTEPS else 0.3
    assert not left
    return table


def kernel(
    r2, w, csel, mask, orb_t, tiles, back,
    big, rg, tbuf, folded, prs, lhs, acc, sendbuf, recvbuf, outbuf,
    tsem, xsend, xrecv, isend, irecv, ssend, srecv, qsend, qrecv, asend, arecv,
):
    me = lax.axis_index("occ")
    q = lax.axis_index("ao")
    z, y, c = me // (2 * YN), (me // 2) % YN, me % 2
    log = route()
    table = slots_of(log)

    def dev(dz, dy, core):
        return (((z + dz + ZN) % ZN) * YN + (y + dy + YN) % YN) * 2 + core

    def occ(i):
        return {"occ": i}

    def ao(d):
        return {"ao": (q + d + XN) % XN}

    def remote(src, dst, ss, rs, to):
        return pltpu.make_async_remote_copy(
            src_ref=src, dst_ref=dst, send_sem=ss, recv_sem=rs, device_id=to, device_id_type=MESH
        )

    sibling = occ(dev(0, 0, 1 - c))

    def wait_recv(ref, sem):
        remote(ref, ref, sem, sem, sibling).wait_recv()

    def wait_send(ref, sem):
        remote(ref, ref, sem, sem, sibling).wait_send()

    load = pltpu.make_async_copy(tiles, tbuf, tsem)
    load.start()

    barrier = pltpu.get_barrier_semaphore()
    for d in range(1, XN):
        pl.semaphore_signal(barrier, inc=1, device_id=ao(d), device_id_type=MESH)

    def greet(d, carry):
        pl.semaphore_signal(
            barrier, inc=1, device_id=occ((me + d) % NDEV), device_id_type=MESH
        )
        return carry

    lax.fori_loop(1, NDEV, greet, 0)
    pl.semaphore_wait(barrier, XN - 1 + NDEV - 1)

    remote(r2, rg.at[3], xsend.at[0], xrecv.at[0], ao(1)).start()
    remote(r2, rg.at[1], xsend.at[1], xrecv.at[1], ao(-1)).start()
    wait_recv(rg.at[3], xrecv.at[0])
    remote(rg.at[3, 0], rg.at[2, 0], xsend.at[2], xrecv.at[2], ao(1)).start()
    wait_recv(rg.at[1], xrecv.at[1])
    remote(rg.at[1, 1], rg.at[2, 1], xsend.at[3], xrecv.at[3], ao(-1)).start()

    def term(block, k):
        return jnp.dot(block, w[k], preferred_element_type=F32)

    for j in range(2):
        part = term(r2[j], 0) + term(rg[3, j], 3) + term(rg[1, j], 1)
        wait_recv(rg.at[2, j], xrecv.at[2 + j])
        part = part + term(rg[2, j], 2)
        big[me, pl.ds(j * 256, 256), :] = part.astype(BF16)

    def piece(dz, dy, cls, part):
        return big.at[dev(dz, dy, c), pl.ds(*extent(cls, part))]

    def handle(event):
        _, part, cls, dz, dy, sends, whole = event
        if part != "own":
            wait_recv(
                piece(dz, dy, cls, part), irecv.at[CLS[cls], dz, dy, 1 if part == "b" else 0]
            )
        for axis, way, out in sends:
            to = occ(dev(way, 0, c) if axis == "z" else dev(0, way, c))
            at = ((dz - way) % ZN, dy) if axis == "z" else (dz, (dy - way) % YN)
            ref = piece(dz, dy, cls, out)
            remote(
                ref, ref, isend, irecv.at[CLS[cls], at[0], at[1], 1 if out == "b" else 0], to
            ).start()
        if whole:
            ref = piece(dz, dy, cls, "f")
            remote(ref, ref, ssend, srecv.at[dz, dy], sibling).start()

    def comm(step, lo, hi):
        if not any(table[lo:hi]):
            return
        if hi - lo == 1:
            for e in table[lo]:
                handle(log[e])
            return
        mid = (lo + hi) // 2

        @pl.when(step < mid)
        def _():
            comm(step, lo, mid)

        @pl.when(step >= mid)
        def _():
            comm(step, mid, hi)

    pairs = SLOTS // 2 // USTEPS

    def fold(step, carry):
        comm(step, 0, USTEPS)

        @pl.when(step == 0)
        def _():
            load.wait()

        for n in range(pairs):
            t = (step * pairs + n) * 2
            two = jnp.concatenate([tbuf[t], tbuf[t + 1]], axis=1)
            res = jnp.dot(orb_t[...], two, preferred_element_type=F32)
            folded[:, pl.ds(pl.multiple_of(t * NU, 256), 256)] = res.astype(BF16)
        return carry

    lax.fori_loop(0, USTEPS, fold, 0)

    row_in = lax.broadcasted_iota(jnp.int32, (GROUP, NU), 0) % 8 < 4
    left = lax.broadcasted_iota(jnp.int32, (GROUP, NU), 1) < 64

    def offset(g):
        return ((g + 1) // 2) * (2 * (g % 2) - 1)

    def finish(g):
        zrow = (z + offset(g) + ZN) % ZN
        wait_recv(recvbuf.at[g], qrecv.at[g])
        v = []
        for lp in range(4):
            total = sendbuf[g, q, lp].astype(F32)
            for k in range(XN - 1):
                total = total + recvbuf[g, k, lp].astype(F32)
            v.append(total)
        even = [
            jnp.where(row_in, v[0], pltpu.roll(v[1], 4, 0)),
            jnp.where(row_in, v[2], pltpu.roll(v[3], 4, 0)),
        ]
        odd = [
            jnp.where(row_in, pltpu.roll(v[0], GROUP - 4, 0), v[1]),
            jnp.where(row_in, pltpu.roll(v[2], GROUP - 4, 0), v[3]),
        ]
        for slot in range(8):
            k8 = slot // 2 * 8
            two = odd if slot % 2 else even
            rows = jnp.concatenate([two[0][k8 : k8 + 8], two[1][k8 : k8 + 8]], axis=0)
            outbuf[g, slot] = rows.astype(BF16)
        for slot in range(8):
            target = zrow * 8 + slot

            @pl.when(target != me)
            def _():
                remote(outbuf.at[g, slot], back.at[me], asend, arecv, occ(target)).start()

            @pl.when(target == me)
            def _():
                back[me] = outbuf[g, slot]

    def group(g, carry):
        dz = (offset(g) + ZN) % ZN
        zrow = (z + dz) % ZN

        def step(k, carry):
            comm(USTEPS + g * GSTEPS + k, USTEPS, len(table))

            @pl.when(k < PSTEPS)
            def _():
                yy = (y + k) % YN
                wait_recv(big.at[(zrow * YN + yy) * 2 + 1 - c], srecv.at[dz, k])
                for core in range(2):
                    slot = yy * 2 + core
                    for j in range(2):
                        res = jnp.dot(
                            csel[...],
                            big[zrow * 8 + slot, pl.ds(j * 256, 256), :],
                            preferred_element_type=F32,
                        )
                        for n in range(2):
                            at = (slot * 4 + 2 * j + n) * SLOTS
                            prs[pl.ds(pl.multiple_of(at, SLOTS), SLOTS), :] = res[
                                :, n * NU : (n + 1) * NU
                            ]

            @pl.when(k >= PSTEPS)
            def _():
                kc = k - PSTEPS
                cols = pl.multiple_of(kc * (8 * NU), 8 * NU)
                m = mask[:, pl.ds(cols, 8 * NU)]
                for t in range(8):
                    x = prs[pl.ds(kc * 8 + t, GROUP, stride=SLOTS), :]
                    for lam in range(8):
                        one = m[lam : lam + 1, t * NU : (t + 1) * NU]
                        lhs[pl.ds(lam * GROUP, GROUP), pl.ds(t * NU, NU)] = (x * one).astype(BF16)
                res = lax.dot_general(
                    lhs[...],
                    folded[:, pl.ds(cols, 8 * NU)],
                    (((1,), (1,)), ((), ())),
                    preferred_element_type=F32,
                )

                @pl.when(kc == 0)
                def _():
                    acc[...] = res

                @pl.when(kc > 0)
                def _():
                    acc[...] += res

            return carry

        lax.fori_loop(0, GSTEPS, step, 0)
        for lp in range(4):
            for h in range(2):
                cols = slice(h * NU, (h + 1) * NU)
                e = acc[pl.ds(2 * lp * GROUP, GROUP), cols]
                o = acc[pl.ds((2 * lp + 1) * GROUP, GROUP), cols]
                sendbuf[g, 2 * h, lp] = jnp.where(left, e, pltpu.roll(o, 64, 1)).astype(BF16)
                sendbuf[g, 2 * h + 1, lp] = jnp.where(left, pltpu.roll(e, 64, 1), o).astype(BF16)
        for k in range(1, XN):
            remote(
                sendbuf.at[g, (q + k) % XN], recvbuf.at[g, XN - 1 - k], qsend, qrecv.at[g], ao(k)
            ).start()

        @pl.when(g > 0)
        def _():
            finish(g - 1)

        return carry

    lax.fori_loop(0, ZN, group, 0)
    finish(ZN - 1)

    wait_send(r2, xsend.at[0])
    wait_send(r2, xsend.at[1])
    wait_send(rg.at[3, 0], xsend.at[2])
    wait_send(rg.at[1, 1], xsend.at[3])
    wait_send(big.at[pl.ds(0, 31)], isend)
    wait_send(big.at[pl.ds(0, 32)], ssend)
    wait_send(recvbuf, qsend)
    wait_send(back.at[pl.ds(0, NDEV - 1)], asend)
    wait_recv(back.at[pl.ds(0, NDEV - 1)], arecv)


def exchange(r2, w, csel, mask, orb_t, tiles):
    vmem = pl.BlockSpec(memory_space=pltpu.VMEM)
    dma = pltpu.SemaphoreType.DMA
    return pl.pallas_call(
        kernel,
        out_shape=jax.ShapeDtypeStruct((NDEV, 16, NU), BF16),
        in_specs=[vmem] * 5 + [pl.BlockSpec(memory_space=pl.ANY)],
        out_specs=vmem,
        scratch_shapes=[
            pltpu.VMEM((NDEV, ROWS, 256), BF16),
            pltpu.VMEM((XN, 2, VIR, NU), BF16),
            pltpu.VMEM((SLOTS, AO, NU), BF16),
            pltpu.VMEM((VIR, SLOTS * NU), BF16),
            pltpu.VMEM((GROUP * SLOTS, NU), F32),
            pltpu.VMEM((8 * GROUP, 8 * NU), BF16),
            pltpu.VMEM((8 * GROUP, VIR), F32),
            pltpu.VMEM((ZN, XN, 4, GROUP, NU), BF16),
            pltpu.VMEM((ZN, XN - 1, 4, GROUP, NU), BF16),
            pltpu.VMEM((ZN, 8, 16, NU), BF16),
            dma(()),
            dma((4,)),
            dma((4,)),
            dma(()),
            dma((2, ZN, YN, 2)),
            dma(()),
            dma((ZN, YN)),
            dma(()),
            dma((ZN,)),
            dma(()),
            dma(()),
        ],
        compiler_params=pltpu.CompilerParams(
            collective_id=0, has_side_effects=True, vmem_limit_bytes=56 * 2**20
        ),
    )(r2, w, csel, mask, orb_t, tiles)


def shards(amplitudes, orbitals, tiles, tile_count, tile_row, tile_src, tile_sub):
    me = lax.axis_index("occ")
    q = lax.axis_index("ao")
    blocks = AO // NDEV
    r2 = jnp.concatenate([amplitudes[0::2], amplitudes[1::2]], axis=2)
    mine = lax.dynamic_slice_in_dim(orbitals, q * NU, NU, 0)
    wt = jnp.roll(mine.T.reshape(XN, VIR // XN, NU), -q, axis=0)
    zero = jnp.zeros_like(wt)
    w = jnp.concatenate(
        [jnp.concatenate([wt, zero], axis=2), jnp.concatenate([zero, wt], axis=2)], axis=1
    )
    src = lax.dynamic_slice_in_dim(tile_src[:, 0], me * SLOTS, SLOTS, 0)
    sub = lax.dynamic_slice_in_dim(tile_sub, me * SLOTS, SLOTS, 0)
    row = lax.dynamic_slice_in_dim(tile_row, me * SLOTS, SLOTS, 0)
    live = jnp.arange(SLOTS, dtype=jnp.int32) < tile_count[me]
    csel = jnp.take(orbitals, src * blocks + sub, axis=0)
    picks = (row[None, :] == jnp.arange(blocks, dtype=jnp.int32)[:, None]) & live[None, :]
    mask = jnp.repeat(picks.astype(F32), NU, axis=1)
    back = exchange(r2, w, csel, mask, orbitals.T, tiles)
    back = back.reshape(NDEV, 4, 4, 2, 64)
    coef = orbitals.reshape(NDEV, 4, 2, VIR)
    return jnp.einsum("olpa,olipb->iab", coef, back, preferred_element_type=F32).astype(BF16)


def solution(mesh):
    placed = (P("occ", None, "ao"), P(), P("occ", None, "ao"), P(), P(), P(), P())
    return jax.shard_map(
        shards, mesh=mesh, in_specs=placed, out_specs=P("occ", None, "ao"), check_vma=False
    )
```

time: 248 us -> 116 us (0.47)
  waiting for transfers between devices: 153 us -> 0 us
  Pallas kernels: 14.1 us -> 101 us
  blocking collectives: 37.5 us -> 0 us
  between operations: 13.5 us -> 0.08 us
  matrix products: 10.9 us -> 1.06 us
  local copies, waits for them, and re-layouts: 16.1 us -> 9.8 us
  other arithmetic: 0.77 us -> 3.66 us
    all_gather x1 -> x0, waiting for transfers between devices: 97.7 us -> none  [shards(): half_all = lax.all_gather(half, 'occ', axis=0, tiled=True)]
    pallas_call x1, Pallas kernels: 14.1 us -> 101 us  [exchange(): pl.pallas_call(kernel, out_shape=jax.ShapeDtypeStruct((NDEV, 16, NU), BF1...]
    reduce_scatter x1 -> x0, waiting for transfers between devices: 55.7 us -> none  [shards(): ladder = lax.psum_scatter(part, 'ao', scatter_dimension=2, tiled=True)]
    all_to_all x1 -> x0, blocking collectives: 25.1 us -> none  [shards(): lax.all_to_all(ladder, 'occ', split_axis=1, concat_axis=0, tiled=True)]
    all_gather x1 -> x0, blocking collectives: 12.5 us -> none  [shards(): amps = lax.all_gather(amplitudes, 'ao', axis=2, tiled=True)]
    dot_general x3 -> x1, matrix products: 10.9 us -> 1.06 us  [shards(): jnp.einsum('olpa,olipb->iab', coef, back, preferred_element_type=F32)]
    dot_general x1 -> x0, local copies, waits for them, and re-layouts: 4.63 us -> none  [shards(): jnp.einsum('tc,icn->tin', chosen, half_all, preferred_element_type=F32)]
    pallas_call x1 -> x0, local copies, waits for them, and re-layouts: 2.64 us -> none  [ladder_rows(): pl.pallas_call(ladder_kernel, out_shape=jax.ShapeDtypeStruct((blocks, occ...]
  transfers between devices with their start and end apart: 2 -> 0, of which waited for: 2 -> 0; matrix products, arithmetic and copies ran while one was open for 3% -> 0% of each run, Pallas kernels for 0% -> 0%
where the time goes in v2:
time: 116 us
  Pallas kernels  101 us (87%)
  local copies, waits for them, and re-layouts  9.8 us (8%)
  other arithmetic  3.66 us (3%)
    pallas_call x1, Pallas kernels, exchange(): pl.pallas_call(kernel, out_shape=jax.ShapeDtypeStruct((NDEV, 16, NU), BF1...  101 us

profile of v2, /device:TPU:1, one launch (start us, length us, event | category | flops | bytes accessed | tf_op | source)
XLA Modules:
  0.0 115.9 jit_solution(3658684648138948175)
XLA Ops:
  0.0 0.0 copy-start
  0.0 0.9 dynamic-slice_bitcast_fusion
  0.9 0.1 copy.16
  1.1 0.7 fusion.5.w
  1.8 0.8 compare_and_fusion
  2.6 1.6 %gather_fusion = bf16[64,256]{1,0:T(8,128)(2,1)S(1)} fusion(bf16[512,256]{1,0:T(8,128)(2,1)} %param.8, s32[1024]{0:T(1024)S(1)} %pad_clamp_fusion), kind=kCustom, calls=%fused_computation | custom fusion | bytes 65792 | tf_op jit(solution)/shard_map/jit(_take)/gather | solution.py:391
  4.2 0.7 broadcast_select_fusion.csel
  4.9 0.8 dynamic_slice.23
  5.7 1.2 %dynamic_slice.24 = s32[1]{0:T(128)} dynamic-slice(s32[64]{0:T(128)} %param.10, s32[]{:T(128)S(6)} %select_n.39), dynamic_slice_sizes={1} | dynamic-slice | bytes 12 | tf_op jit(solution)/shard_map/dynamic_slice | solution.py:390
  6.9 0.6 iota_compare_fusion.3
  7.6 0.1 copy.17
  7.7 0.8 broadcast_bitcast_fusion.mask
  8.5 0.9 fusion.14
  9.4 0.1 copy.22
  9.5 0.1 copy.23
  9.7 0.8 pad_maximum_fusion.r2
  10.4 1.8 %copy.18 = bf16[512,256]{0,1:T(8,128)(2,1)} copy(bf16[512,256]{1,0:T(8,128)(2,1)} %param.8) | data formatting | bytes 524288 | tf_op args[1]
  12.2 101.3 %shard_map.73 = bf16[64,16,128]{2,1,0:T(8,128)(2,1)} custom-call(bf16[2,256,128]{2,1,0:T(8,128)(2,1)} %pad_maximum_fusion.r2, bf16[4,128,256]{2,1,0:T(8,128)(2,1)} %fusion.5.w, bf16[64,256]{1,0:T(8,128)(2,1)} %broadcast_select_fusion.csel, f32[8,8192]{1,0:T(8,128)} %broadcast_bitcast_fusion.mask, bf16[256,512]{1,0:T(8,128)(2,1)} %bitcast.27, ...), custom_call_target="tpu_custom_call" | custom-call | tf_op jit(solution)/shard_map/pallas_call | solution.py:342
  113.5 1.2 %reshape.27 = bf16[64,4,4,2,64]{4,3,2,1,0:T(2,128)(2,1)S(1)} reshape(bf16[64,16,128]{2,1,0:T(8,128)(2,1)} %shard_map.73) | data formatting | bytes 524288 | tf_op jit(solution)/shard_map/reshape | solution.py:395
  114.7 0.0 copy-done
  114.8 0.1 reshape.28
  114.9 1.1 fusion.1
  (3 shorter events, 0.1 us)
Async XLA Ops:
  0.0 114.7 %copy-start = (bf16[512,256]{1,0:T(8,128)(2,1)S(1)}, bf16[512,256]{1,0:T(8,128)(2,1)}, u32[]{:S(2)}) copy-start(bf16[512,256]{1,0:T(8,128)(2,1)} %param.8) | copy-start | bytes 786436

commit v3 on v2

v3 whole, which is shorter than its diff:
```python
import functools
import heapq
import itertools

import jax
import jax.numpy as jnp
from jax import lax
from jax.experimental import pallas as pl
from jax.experimental.pallas import tpu as pltpu
from jax.sharding import PartitionSpec as P

BF16, F32 = jnp.bfloat16, jnp.float32
MESH = pl.DeviceIdType.MESH
ZN, YN, XN = 8, 4, 4
NDEV = ZN * YN * 2
ROWS, WIDTH = 256, 512
CUT = {"P": (0, 80, 160), "Q": (160, 208, 256)}
CLS = {"P": 0, "Q": 1}
GROUPS = 8
ROW_ORDER = (0, 1, 7, 2, 6, 3, 5, 4)
SLOTS, NU, AO, VIR = 64, 128, 512, 256
USTEPS, PSTEPS, KSTEPS = 8, 4, 8
EARLY, EARLY2, FOLDS = 8, 16, 2
GSTEPS = PSTEPS + KSTEPS
GROUP = 32


def extent(cls, part):
    lo, mid, hi = CUT[cls]
    return {"f": (lo, hi - lo), "a": (lo, mid - lo), "b": (mid, hi - mid)}[part]


def route(rate=91e3, latency=1.7):
    free = {("z", 1): 0.0, ("z", -1): 0.0, ("y", 1): 0.0, ("y", -1): 0.0}
    tick = itertools.count()
    events, log, halves = [], [], {}

    def emit(now, cls, dz, dy, sends):
        for axis, way, part in sends:
            start = max(now, free[axis, way])
            free[axis, way] = start + 2 * 2 * WIDTH * extent(cls, part)[1] / rate
            at = ((dz - way) % ZN, dy) if axis == "z" else (dz, (dy - way) % YN)
            heapq.heappush(
                events, (free[axis, way] + latency, next(tick), cls, *at, part, axis, way)
            )

    for cls, axis in (("P", "z"), ("Q", "y"), ("P", "y"), ("Q", "z")):
        sends = [(axis, 1, "f"), (axis, -1, "f")]
        log.append((0.0, "own", cls, 0, 0, sends, axis == ("z" if cls == "P" else "y")))
        emit(0.0, cls, 0, 0, sends)
    while events:
        now, _, cls, dz, dy, part, axis, way = heapq.heappop(events)
        n = ZN if axis == "z" else YN
        gone = (-way * (dz if axis == "z" else dy)) % n
        sends = []
        if gone < n // 2 - 1:
            sends.append((axis, way, "f"))
        elif gone == n // 2 - 1:
            sends.append((axis, way, "a" if way == 1 else "b"))
        whole = part == "f"
        if not whole:
            seen = halves.setdefault((cls, dz, dy), set())
            seen.add(part)
            whole = len(seen) == 2
        if whole and axis == ("z" if cls == "P" else "y"):
            other = "y" if cls == "P" else "z"
            sends += [(other, 1, "f"), (other, -1, "f")]
        log.append((now, part, cls, dz, dy, sends, whole))
        emit(now, cls, dz, dy, sends)
    return log


def order_of(log):
    whole = {}
    for now, _, _, dz, dy, _, _ in log:
        whole[dz * YN + dy] = max(now, whole.get(dz * YN + dy, 0.0))
    return [dz * YN + dy for dz in ROW_ORDER for dy in range(YN)], whole


def slots_of(log):
    table = [[] for _ in range(USTEPS + GROUPS * GSTEPS)]
    order, whole = order_of(log)
    now, left = 0.0, list(range(len(log)))

    def take(step, test):
        nonlocal left
        table[step] += [e for e in left if test(log[e])]
        left = [e for e in left if not test(log[e])]

    for step in range(USTEPS):
        take(step, lambda e: e[0] <= now)
        now += 0.8
    for g in range(GROUPS):
        for k in range(GSTEPS):
            if k < PSTEPS:
                now = max(now, whole[order[g * 4 + k]])
            take(USTEPS + g * GSTEPS + k, lambda e: e[0] <= now)
            now += 0.5 if k < PSTEPS else 0.3
    assert not left
    return table


def kernel(
    amps, orb, src, sub, row, count, tiles, back,
    big, rg, tbuf, folded, prs, acc, sendbuf, recvbuf, outbuf, orb_t, csel, pick,
    tsem, xsend, xrecv, isend, irecv, ssend, srecv, qsend, qrecv, asend, arecv,
):
    me = lax.axis_index("occ")
    q = lax.axis_index("ao")
    z, y, c = me // (2 * YN), (me // 2) % YN, me % 2
    log = route()
    table = slots_of(log)

    def dev(dz, dy, core):
        return (((z + dz + ZN) % ZN) * YN + (y + dy + YN) % YN) * 2 + core

    def occ(i):
        return {"occ": i}

    def ao(d):
        return {"ao": (q + d + XN) % XN}

    def remote(src, dst, ss, rs, to):
        return pltpu.make_async_remote_copy(
            src_ref=src, dst_ref=dst, send_sem=ss, recv_sem=rs, device_id=to, device_id_type=MESH
        )

    sibling = occ(dev(0, 0, 1 - c))

    def wait_recv(ref, sem):
        remote(ref, ref, sem, sem, sibling).wait_recv()

    def wait_send(ref, sem):
        remote(ref, ref, sem, sem, sibling).wait_send()

    load = pltpu.make_async_copy(tiles, tbuf, tsem)
    load.start()

    barrier = pltpu.get_barrier_semaphore()
    for d in range(1, XN):
        pl.semaphore_signal(barrier, inc=1, device_id=ao(d), device_id_type=MESH)

    def greet(d, carry):
        pl.semaphore_signal(
            barrier, inc=1, device_id=occ((me + d) % NDEV), device_id_type=MESH
        )
        return carry

    lax.fori_loop(1, NDEV, greet, 0)

    orb_t[...] = orb[...].astype(F32).T.astype(BF16)

    def own_slots(ref):
        v = ref[pl.ds(me // 2, 1), :].astype(F32)
        return jnp.where(c == 1, pltpu.roll(v, 64, 1), v)

    block = own_slots(src) * 8.0 + own_slots(sub)
    block = jnp.broadcast_to(block, (128, 128)).T[:SLOTS]
    lane = lax.broadcasted_iota(jnp.int32, (SLOTS, 128), 1).astype(F32)
    chosen = jnp.concatenate(
        [(block == lane + 128.0 * n).astype(F32).astype(BF16) for n in range(4)], axis=1
    )
    csel[...] = jnp.dot(chosen, orb[...], preferred_element_type=F32).astype(BF16)

    def choose(t, carry):
        r = jnp.where(t < count[me], row[me // 2, c * SLOTS + t], 8)
        for lam in range(8):
            pick[lam, t] = jnp.where(r == lam, 1.0, 0.0)
        return carry

    lax.fori_loop(0, SLOTS, choose, 0)
    pl.semaphore_wait(barrier, XN - 1 + NDEV - 1)

    def quarter(d, lo, n):
        return rg.at[(q + d + XN) % XN, pl.ds(lo, n)]

    front, rear = pl.ds(0, 2), pl.ds(2, 2)
    remote(amps.at[front], quarter(0, 0, 2), xsend.at[0], xrecv.at[0], ao(1)).start()
    remote(amps.at[rear], quarter(0, 2, 2), xsend.at[1], xrecv.at[1], ao(-1)).start()
    remote(amps.at[rear], quarter(0, 2, 2), xsend.at[4], xrecv.at[4], ao(1)).start()
    remote(amps.at[front], quarter(0, 0, 2), xsend.at[5], xrecv.at[5], ao(-1)).start()
    rg[q] = amps[...]

    load.wait()

    def fold(step, carry):
        t = step * 2
        two = jnp.concatenate([tbuf[t], tbuf[t + 1]], axis=1)
        res = jnp.dot(orb_t[...], two, preferred_element_type=F32)
        folded[pl.ds(pl.multiple_of(t * NU, 256), 256), :] = res.T.astype(BF16)
        return carry

    lax.fori_loop(0, EARLY, fold, 0)

    wait_recv(quarter(-1, 0, 2), xrecv.at[0])
    remote(quarter(-1, 0, 2), quarter(-1, 0, 2), xsend.at[2], xrecv.at[2], ao(1)).start()
    wait_recv(quarter(1, 2, 2), xrecv.at[1])
    remote(quarter(1, 2, 2), quarter(1, 2, 2), xsend.at[3], xrecv.at[3], ao(-1)).start()
    lax.fori_loop(EARLY, EARLY2, fold, 0)
    mine = orb[pl.ds(pl.multiple_of(q * NU, NU), NU), :]
    wait_recv(quarter(-1, 2, 2), xrecv.at[4])
    wait_recv(quarter(1, 0, 2), xrecv.at[5])
    for j in range(2):
        wait_recv(quarter(2, 2 * j, 2), xrecv.at[2 + j])
        for i in (2 * j, 2 * j + 1):
            whole = jnp.concatenate([rg[k, i] for k in range(XN)], axis=0)
            part = jnp.dot(mine, whole, preferred_element_type=F32)
            big[me, :, pl.ds(i * NU, NU)] = part.T.astype(BF16)

    def piece(dz, dy, cls, part):
        return big.at[dev(dz, dy, c), pl.ds(*extent(cls, part))]

    def handle(event):
        _, part, cls, dz, dy, sends, whole = event
        if part != "own":
            wait_recv(
                piece(dz, dy, cls, part), irecv.at[CLS[cls], dz, dy, 1 if part == "b" else 0]
            )
        for axis, way, out in sends:
            to = occ(dev(way, 0, c) if axis == "z" else dev(0, way, c))
            at = ((dz - way) % ZN, dy) if axis == "z" else (dz, (dy - way) % YN)
            ref = piece(dz, dy, cls, out)
            remote(
                ref, ref, isend, irecv.at[CLS[cls], at[0], at[1], 1 if out == "b" else 0], to
            ).start()
        if whole:
            ref = piece(dz, dy, cls, "f")
            remote(ref, ref, ssend, srecv.at[dz, dy], sibling).start()

    def comm(step, lo, hi):
        if not any(table[lo:hi]):
            return
        if hi - lo == 1:
            for e in table[lo]:
                handle(log[e])
            return
        mid = (lo + hi) // 2

        @pl.when(step < mid)
        def _():
            comm(step, lo, mid)

        @pl.when(step >= mid)
        def _():
            comm(step, mid, hi)

    def fold_rest(step, carry):
        comm(step, 0, USTEPS)
        lax.fori_loop(EARLY2 + step * FOLDS, EARLY2 + (step + 1) * FOLDS, fold, 0)
        return carry

    lax.fori_loop(0, USTEPS, fold_rest, 0)

    row_in = lax.broadcasted_iota(jnp.int32, (GROUP, NU), 0) % 8 < 4
    left = lax.broadcasted_iota(jnp.int32, (GROUP, NU), 1) < 64

    def offset(g):
        return (((g + 1) // 2) * (2 * (g % 2) - 1) + ZN) % ZN

    def finish(g):
        wait_recv(recvbuf.at[g], qrecv.at[g])
        v = []
        for lp in range(4):
            total = sendbuf[g, q, lp].astype(F32)
            for k in range(XN - 1):
                total = total + recvbuf[g, k, lp].astype(F32)
            v.append(total)
        even = [
            jnp.where(row_in, v[0], pltpu.roll(v[1], 4, 0)),
            jnp.where(row_in, v[2], pltpu.roll(v[3], 4, 0)),
        ]
        odd = [
            jnp.where(row_in, pltpu.roll(v[0], GROUP - 4, 0), v[1]),
            jnp.where(row_in, pltpu.roll(v[2], GROUP - 4, 0), v[3]),
        ]
        for slot in range(8):
            k8 = slot // 2 * 8
            two = odd if slot % 2 else even
            rows = jnp.concatenate([two[0][k8 : k8 + 8], two[1][k8 : k8 + 8]], axis=0)
            outbuf[g, slot] = rows.astype(BF16)
        dz = offset(g)
        for slot in range(8):
            target = dev(dz, slot // 2, slot % 2)

            @pl.when(target != me)
            def _():
                remote(outbuf.at[g, slot], back.at[me], asend, arecv, occ(target)).start()

            @pl.when(target == me)
            def _():
                back[me] = outbuf[g, slot]

    def group(g, carry):
        dz = offset(g)

        def step(k, carry):
            comm(USTEPS + g * GSTEPS + k, USTEPS, len(table))

            @pl.when(k < PSTEPS)
            def _():
                dy = k
                wait_recv(big.at[dev(dz, dy, 1 - c)], srecv.at[dz, dy])
                for core in range(2):
                    slot = k * 2 + core
                    res = jnp.dot(
                        csel[...], big[dev(dz, dy, core)], preferred_element_type=F32
                    )
                    for n in range(4):
                        at = (slot * 4 + n) * SLOTS
                        prs[pl.ds(pl.multiple_of(at, SLOTS), SLOTS), :] = res[
                            :, n * NU : (n + 1) * NU
                        ]

            @pl.when(k >= PSTEPS)
            def _():
                kc = k - PSTEPS
                outs = []
                for n in range(8):
                    t = kc * 8 + n
                    x = prs[pl.ds(t, GROUP, stride=SLOTS), :].astype(BF16)
                    rows = folded[pl.ds(pl.multiple_of(t * NU, NU), NU), :]
                    outs.append(jnp.dot(x, rows, preferred_element_type=F32))
                for lam in range(8):
                    total = outs[0] * pick[lam, kc * 8]
                    for n in range(1, 8):
                        total = total + outs[n] * pick[lam, kc * 8 + n]
                    acc[lam] += total

            return carry

        acc[...] = jnp.zeros_like(acc)
        lax.fori_loop(0, GSTEPS, step, 0)
        for lp in range(4):
            for h in range(2):
                cols = slice(h * NU, (h + 1) * NU)
                e = acc[2 * lp, :, cols]
                o = acc[2 * lp + 1, :, cols]
                sendbuf[g, 2 * h, lp] = jnp.where(left, e, pltpu.roll(o, 64, 1)).astype(BF16)
                sendbuf[g, 2 * h + 1, lp] = jnp.where(left, pltpu.roll(e, 64, 1), o).astype(BF16)
        for k in range(1, XN):
            remote(
                sendbuf.at[g, (q + k) % XN], recvbuf.at[g, XN - 1 - k], qsend, qrecv.at[g], ao(k)
            ).start()

        @pl.when(g > 0)
        def _():
            finish(g - 1)

        return carry

    lax.fori_loop(0, GROUPS, group, 0)
    finish(GROUPS - 1)

    for n in (0, 1, 4, 5):
        wait_send(amps.at[front], xsend.at[n])
    wait_send(quarter(-1, 0, 2), xsend.at[2])
    wait_send(quarter(1, 2, 2), xsend.at[3])
    wait_send(big.at[pl.ds(0, 31)], isend)
    wait_send(big.at[pl.ds(0, 32)], ssend)
    wait_send(recvbuf, qsend)
    wait_send(back.at[pl.ds(0, NDEV - 1)], asend)
    wait_recv(back.at[pl.ds(0, NDEV - 1)], arecv)


def exchange(amps, orb, src, sub, row, count, tiles):
    vmem = pl.BlockSpec(memory_space=pltpu.VMEM)
    dma = pltpu.SemaphoreType.DMA
    return pl.pallas_call(
        kernel,
        out_shape=jax.ShapeDtypeStruct((NDEV, 16, NU), BF16),
        in_specs=[vmem] * 4
        + [pl.BlockSpec(memory_space=pltpu.SMEM)] * 2
        + [pl.BlockSpec(memory_space=pl.ANY)],
        out_specs=vmem,
        scratch_shapes=[
            pltpu.VMEM((NDEV, ROWS, WIDTH), BF16),
            pltpu.VMEM((XN, 4, VIR // XN, VIR), BF16),
            pltpu.VMEM((SLOTS, AO, NU), BF16),
            pltpu.VMEM((SLOTS * NU, VIR), BF16),
            pltpu.VMEM((GROUP * SLOTS, NU), F32),
            pltpu.VMEM((8, GROUP, VIR), F32),
            pltpu.VMEM((ZN, XN, 4, GROUP, NU), BF16),
            pltpu.VMEM((ZN, XN - 1, 4, GROUP, NU), BF16),
            pltpu.VMEM((ZN, 8, 16, NU), BF16),
            pltpu.VMEM((VIR, AO), BF16),
            pltpu.VMEM((SLOTS, VIR), BF16),
            pltpu.SMEM((8, SLOTS), F32),
            dma(()),
            dma((6,)),
            dma((6,)),
            dma(()),
            dma((2, ZN, YN, 2)),
            dma(()),
            dma((ZN, YN)),
            dma(()),
            dma((ZN,)),
            dma(()),
            dma(()),
        ],
        compiler_params=pltpu.CompilerParams(
            collective_id=0, has_side_effects=True, vmem_limit_bytes=56 * 2**20
        ),
    )(amps, orb, src, sub, row, count, tiles)


def shards(amplitudes, orbitals, tiles, tile_count, tile_row, tile_src, tile_sub):
    back = exchange(
        amplitudes.transpose(0, 2, 1),
        orbitals,
        tile_src.reshape(32, 128),
        tile_sub.reshape(32, 128),
        tile_row.reshape(32, 128),
        tile_count,
        tiles,
    )
    back = back.reshape(NDEV, 4, 4, 2, 64)
    coef = orbitals.reshape(NDEV, 4, 2, VIR)
    return jnp.einsum("olpa,olipb->iab", coef, back, preferred_element_type=F32).astype(BF16)


def solution(mesh):
    placed = (P("occ", None, "ao"), P(), P("occ", None, "ao"), P(), P(), P(), P())
    return jax.shard_map(
        shards, mesh=mesh, in_specs=placed, out_specs=P("occ", None, "ao"), check_vma=False
    )
```

time: 116 us -> 98.6 us (0.85)
  local copies, waits for them, and re-layouts: 9.8 us -> 1.3 us
  Pallas kernels: 101 us -> 96 us
  other arithmetic: 3.66 us -> 0 us
    pallas_call x1, Pallas kernels: 101 us -> 96 us  [exchange(): pl.pallas_call(kernel, out_shape=jax.ShapeDtypeStruct((NDEV, 16, NU), BF1...]
    unnamed x5 -> x2, local copies, waits for them, and re-layouts: 2.03 us -> 0.01 us
    dynamic_slice x2 -> x0, local copies, waits for them, and re-layouts: 2 us -> none  [the longest x1 1.24 us: shards(): live = jnp.arange(SLOTS, dtype=jnp.int32) < tile_count[me]]
    gather x1 -> x0, local copies, waits for them, and re-layouts: 1.64 us -> none  [shards(): csel = jnp.take(orbitals, src * blocks + sub, axis=0)]
    concatenate x3 -> x0, other arithmetic: 1.53 us -> none  [the longest x1 0.77 us: shards(): r2 = jnp.concatenate([amplitudes[0::2], amplitudes[1::2]], axis=2)]
where the time goes in v3:
time: 98.6 us; the launch traced here: 98.4 us
  Pallas kernels  96 us (97%)
  local copies, waits for them, and re-layouts  1.3 us (1%)
  matrix products  1.06 us (1%)
    pallas_call x1, Pallas kernels, exchange(): pl.pallas_call(kernel, out_shape=jax.ShapeDtypeStruct((NDEV, 16, NU), BF1...  96 us

profile of v3, /device:TPU:1, one launch (start us, length us, event | category | flops | bytes accessed | tf_op | source)
XLA Modules:
  0.0 98.4 jit_solution(14880876524086168151)
XLA Ops:
  0.0 0.0 copy-start
  0.0 96.0 %shard_map.73 = bf16[64,16,128]{2,1,0:T(8,128)(2,1)} custom-call(bf16[4,64,256]{2,1,0:T(8,128)(2,1)} %bitcast.17, bf16[512,256]{1,0:T(8,128)(2,1)} %orb.1, s32[32,128]{1,0:T(8,128)} %bitcast.18, s32[32,128]{1,0:T(8,128)} %bitcast.19, s32[32,128]{1,0:T(8,128)} %bitcast.20, s32[64]{0:T(128)} %count.1, bf16[64,512,128]{2,1,0:T(8,128)(2,1)} %tiles.1), custom_call_target="tpu_custom_call" | custom-call | tf_op jit(solution)/shard_map/pallas_call | solution.py:368
  96.0 1.2 %reshape.18 = bf16[64,4,4,2,64]{4,3,2,1,0:T(2,128)(2,1)S(1)} reshape(bf16[64,16,128]{2,1,0:T(8,128)(2,1)} %shard_map.73) | data formatting | bytes 524288 | tf_op jit(solution)/shard_map/reshape | solution.py:416
  97.2 0.0 copy-done
  97.2 0.1 reshape.19
  97.3 1.1 %fusion.1 = bf16[4,256,64]{1,2,0:T(8,128)(2,1)} fusion(bf16[64,4,4,2,64]{4,3,2,1,0:T(2,128)(2,1)S(1)} %reshape.18, bf16[64,4,2,256]{3,2,1,0:T(2,128)(2,1)S(1)} %reshape.19), kind=kOutput, calls=%fused_computation.2 | convolution fusion | flops 67174400 | bytes 655360 | tf_op jit(solution)/shard_map/olpa,olipb->iab/dot_general | solution.py:418
Async XLA Ops:
  0.0 97.2 %copy-start = (bf16[512,256]{1,0:T(8,128)(2,1)S(1)}, bf16[512,256]{1,0:T(8,128)(2,1)}, u32[]{:S(2)}) copy-start(bf16[512,256]{1,0:T(8,128)(2,1)} %orb.1) | copy-start | bytes 786436
